TPU v7x, 256 devices: a whole 4x4x8 slice. The times are simulated.
256 devices in a mesh: row: 16 (over z, x_lo), col: 16 (over y, x_hi, core).
Axes of the slice: x: 4 (x_hi: 2, x_lo: 2; x = x_hi * 2 + x_lo), y: 4, z: 8, core: 2. Of those that a mesh axis runs over, the one named last changes fastest.
Arguments:
- fock_matrix: bfloat16 [12288, 12288], P('row', 'col'), as said below
- density: bfloat16 [12288, 12288], P('row', 'col'), as said below
- intersection: bfloat16 [12288, 12288], P('row', 'col'), as said below
- pattern: int32 [96, 96], replicated, may hold values from 0 to 1, as said below
Outputs:
- gradient_panel: bfloat16 [12288, 2048], P('row', 'col')
Inputs may be any that keep to these rules, and one draw needn't show every extreme that they name: `pattern`: symmetric, with ones on the diagonal; pattern[i, j] is 1 exactly where the centres of blocks i and j lie within the neighbour cutoff of each other. `fock_matrix`: symmetric; zero in every block (i, j) with pattern[i, j] == 0. `density`: symmetric; zero in every block (i, j) with pattern[i, j] == 0. `intersection`: symmetric; zero in every block (i, j) with pattern[i, j] == 0.
All inputs are finite; a program needn't handle non-finite values.
Results may differ from a plain program's by a relative error of at most 0.023.
Values may be sent and summed in bfloat16 or wider, within the bound.
A program may use at most 128 MiB of HBM per device.

v0:
```python
import jax
import jax.numpy as jnp
from jax import lax
from jax.sharding import PartitionSpec as P

BLK = 128


def local(fock_matrix, density, intersection, pattern):
    col_index = lax.axis_index("col")
    tile_rows, tile_cols = fock_matrix.shape
    blocks_col = tile_cols // BLK
    panel_local = jnp.stack([intersection[:, :BLK], fock_matrix[:, :BLK]])
    row_partials = jnp.einsum(
        "ki,skp->sip",
        density,
        lax.all_gather(panel_local, "col", axis=2, tiled=True),
        preferred_element_type=jnp.float32,
    )
    panel_width = row_partials.shape[2]
    owned_blocks = lax.dynamic_slice_in_dim(pattern, col_index * blocks_col, blocks_col, 0)[
        :, ::blocks_col
    ]
    keep_mask = jnp.broadcast_to(
        owned_blocks.astype(jnp.float32)[:, None, :, None],
        (blocks_col, BLK, owned_blocks.shape[1], BLK),
    ).reshape(tile_cols, panel_width)
    combined = lax.psum(row_partials.astype(jnp.bfloat16), "row").astype(jnp.float32)
    filtered = (combined * keep_mask[None]).astype(jnp.bfloat16)
    column_term = jnp.dot(fock_matrix, filtered[0], preferred_element_type=jnp.float32)
    column_term = column_term - jnp.dot(
        intersection, filtered[1], preferred_element_type=jnp.float32
    )
    return lax.psum_scatter(
        column_term.astype(jnp.bfloat16), "col", scatter_dimension=1, tiled=True
    )


def solution(mesh):
    return jax.shard_map(
        local,
        mesh=mesh,
        in_specs=(P("row", "col"), P("row", "col"), P("row", "col"), P()),
        out_specs=P("row", "col"),
        check_vma=False,
    )
```

profile of v0, /device:TPU:1, one launch (start us, length us, event | category | flops | bytes accessed | tf_op | source)
XLA Modules:
  0.0 481.8 jit_solution(13129948686597280517)
XLA Ops:
  6.5 0.0 copy-start
  6.5 0.0 all-gather.2.cloned.1.call-start
  6.5 1.0 slice.16
  7.6 0.1 copy.14
  7.7 0.9 slice.15
  8.7 0.1 copy.13
  8.8 0.8 pad_maximum_fusion
  9.6 0.0 all-gather.2.cloned.1.call-update
  9.6 0.0 all-reduce.2.cloned.1.call-start
  9.7 73.9 %all-gather.2.cloned.1.call-done = bf16[2,768,2048]{1,2,0:T(8,128)(2,1)} async-done(((bf16[2,768,128]{1,2,0:T(8,128)(2,1)}), bf16[2,768,2048]{1,2,0:T(8,128)(2,1)}) %all-gather.2.cloned.1.call-update) | async-done | bytes 6291472 | tf_op jit(solution)/shard_map/all_gather | solution.py:17
  83.6 0.0 copy-done
  83.6 9.7 %convert_bitcast_fusion = bf16[2,768,2048]{1,2,0:T(8,128)(2,1)} fusion(bf16[2,768,2048]{1,2,0:T(8,128)(2,1)} %all-gather.2.cloned.1.call-done, bf16[768,768]{1,0:T(8,128)(2,1)S(1)} %copy-done), kind=kOutput, calls=%fused_computation.3 | convolution fusion | flops 4834983936 | bytes 13762560 | tf_op jit(solution)/shard_map/ki,skp->sip/dot_general | solution.py:14
  93.3 0.0 all-reduce.2.cloned.1.call-update
  93.3 0.0 reduce-scatter.2.cloned.1.call-start
  93.4 0.7 constant_dynamic-slice_fusion
  94.1 0.1 slice.17
  94.2 0.5 broadcast_in_dim.2
  94.7 5.6 %copy.17 = f32[96,8,16,128]{3,1,2,0:T(8,128)} copy(f32[96,8,16,128]{3,2,1,0:T(8,128)S(1)} %bitcast.25) | data formatting | bytes 12582912
  100.3 6.6 %copy.11 = f32[768,2048]{0,1:T(8,128)} copy(f32[768,2048]{1,0:T(8,128)} %bitcast.26) | data formatting | bytes 12582912 | tf_op jit(solution)/shard_map/mul | solution.py:29
  106.9 0.0 copy-start.2
  106.9 266.3 %all-reduce.2.cloned.1.call-done = bf16[2,768,2048]{1,2,0:T(8,128)(2,1)} async-done(((bf16[2,768,2048]{1,2,0:T(8,128)(2,1)}), bf16[2,768,2048]{1,2,0:T(8,128)(2,1)}) %all-reduce.2.cloned.1.call-update) | async-done | bytes 6291472 | tf_op jit(solution)/shard_map/psum | solution.py:28
  373.2 8.4 %multiply_convert_fusion = bf16[2,768,2048]{1,2,0:T(8,128)(2,1)} fusion(bf16[2,768,2048]{1,2,0:T(8,128)(2,1)} %all-reduce.2.cloned.1.call-done, f32[768,2048]{0,1:T(8,128)} %copy.11), kind=kLoop, calls=%fused_computation | loop fusion | flops 9437184 | bytes 18874368 | tf_op jit(solution)/shard_map/convert_element_type | solution.py:29
  381.6 0.0 copy-done.2
  381.6 0.0 copy-start.1
  381.6 0.0 copy-start.3
  381.6 4.7 fusion
  386.4 0.0 copy-done.1
  386.4 0.0 copy-done.3
  386.4 4.1 fusion.1
  390.4 0.0 reduce-scatter.2.cloned.1.call-update
  390.5 83.1 %reduce-scatter.2.cloned.1.call-done = bf16[768,128]{0,1:T(8,128)(2,1)} async-done(((bf16[768,2048]{0,1:T(8,128)(2,1)}), bf16[768,128]{0,1:T(8,128)(2,1)}) %reduce-scatter.2.cloned.1.call-update) | async-done | bytes 196624 | tf_op jit(solution)/shard_map/reduce_scatter | solution.py:34
  473.5 1.7 copy.12
  (1 shorter events, 0.0 us)
Async XLA Ops:
  6.5 77.0 %copy-start = (bf16[768,768]{1,0:T(8,128)(2,1)S(1)}, bf16[768,768]{1,0:T(8,128)(2,1)}, u32[]{:S(2)}) copy-start(bf16[768,768]{1,0:T(8,128)(2,1)} %param.5) | copy-start | bytes 3538948
  6.5 77.0 %all-gather.2.cloned.1.call-start = ((), (), s32[]{:S(2)}) async-start(), calls=%async_computation.1 | async-start | bytes 6684672 | tf_op jit(solution)/shard_map/all_gather | solution.py:17
  9.6 363.6 %all-reduce.2.cloned.1.call-start = ((), (), s32[]{:S(2)}) async-start(), calls=%async_computation.2 | async-start | bytes 12582912 | tf_op jit(solution)/shard_map/psum | solution.py:28
  93.3 380.2 %reduce-scatter.2.cloned.1.call-start = ((), (), s32[]{:S(2)}) async-start(), calls=%async_computation.3 | async-start | bytes 3342336 | tf_op jit(solution)/shard_map/reduce_scatter | solution.py:34
  106.9 274.7 %copy-start.2 = (bf16[768,768]{1,0:T(8,128)(2,1)S(1)}, bf16[768,768]{1,0:T(8,128)(2,1)}, u32[]{:S(2)}) copy-start(bf16[768,768]{1,0:T(8,128)(2,1)} %param.4) | copy-start | bytes 3538948
  381.6 4.8 copy-start.1
  381.6 4.8 copy-start.3
Sparse Core Ops, SparseCore 0:
  10.2 73.3 all-gather.1
  93.4 279.7 all-reduce.1
  390.6 82.8 reduce-scatter.1
where the time goes:
time: 482 us
  waiting for transfers between devices  423 us (88%)
  matrix products  18.6 us (4%)
  local copies, waits for them, and re-layouts  17.5 us (4%)
  between operations  13.2 us (3%)
  other arithmetic  9.15 us (2%)
    psum x1, waiting for transfers between devices, local(): lax.psum(row_partials.astype(jnp.bfloat16), 'row').astype(jnp.float32)  266 us
    reduce_scatter x1, waiting for transfers between devices, local(): lax.psum_scatter(column_term.astype(jnp.bfloat16), 'col', scatter_dimensi...  83.1 us
    all_gather x1, waiting for transfers between devices, local(): lax.all_gather(panel_local, 'col', axis=2, tiled=True)  73.9 us
    dot_general x1, matrix products, local(): jnp.einsum('ki,skp->sip', density, lax.all_gather(panel_local, 'col', axi...  9.74 us
  transfers between devices with their start and end apart: 3, of which 3 were waited for; matrix products, arithmetic and copies ran while one was open for 3% of the time, Pallas kernels for 0%

commit v1 on v0

--- a/solution.py
+++ b/solution.py
@@ -4,6 +4,11 @@
 from jax.sharding import PartitionSpec as P
 
 BLK = 128
+
+
+def gather_and_add(array, mesh_axis):
+    terms = lax.all_gather(array, mesh_axis)
+    return jnp.sum(terms, axis=0)
 
 
 def local(fock_matrix, density, intersection, pattern):
@@ -25,7 +30,7 @@
         owned_blocks.astype(jnp.float32)[:, None, :, None],
         (blocks_col, BLK, owned_blocks.shape[1], BLK),
     ).reshape(tile_cols, panel_width)
-    combined = lax.psum(row_partials.astype(jnp.bfloat16), "row").astype(jnp.float32)
+    combined = gather_and_add(row_partials.astype(jnp.bfloat16), "row").astype(jnp.float32)
     filtered = (combined * keep_mask[None]).astype(jnp.bfloat16)
     column_term = jnp.dot(fock_matrix, filtered[0], preferred_element_type=jnp.float32)
     column_term = column_term - jnp.dot(

time: 482 us -> 2290 us (4.75)
  waiting for transfers between devices: 423 us -> 2180 us
  other arithmetic: 9.15 us -> 44 us
    all_gather x0 -> x1, waiting for transfers between devices: none -> 2020 us  [gather_and_add(): terms = lax.all_gather(array, mesh_axis)]
    psum x1 -> x0, waiting for transfers between devices: 266 us -> none  [local(): lax.psum(row_partials.astype(jnp.bfloat16), 'row').astype(jnp.float32)]
    reduce_sum x0 -> x1, other arithmetic: none -> 34.7 us  [gather_and_add(): return jnp.sum(terms, axis=0)]
  transfers between devices with their start and end apart: 3 -> 3, of which waited for: 3 -> 3; matrix products, arithmetic and copies ran while one was open for 3% -> 1% of each run, Pallas kernels for 0% -> 0%
where the time goes in v1:
time: 2290 us
  waiting for transfers between devices  2180 us (95%)
  other arithmetic  44 us (2%)
  local copies, waits for them, and re-layouts  35 us (2%)
    all_gather x1, waiting for transfers between devices, gather_and_add(): terms = lax.all_gather(array, mesh_axis)  2020 us
    reduce_scatter x1, waiting for transfers between devices, local(): lax.psum_scatter(column_term.astype(jnp.bfloat16), 'col', scatter_dimensi...  82.9 us
    all_gather x1, waiting for transfers between devices, local(): lax.all_gather(panel_local, 'col', axis=2, tiled=True)  73.9 us
  transfers between devices with their start and end apart: 3, of which 3 were waited for; matrix products, arithmetic and copies ran while one was open for 1% of the time, Pallas kernels for 0%

profile of v1, /device:TPU:1, one launch (start us, length us, event | category | flops | bytes accessed | tf_op | source)
XLA Modules:
  0.0 2287.9 jit_solution(5033939473639731193)
XLA Ops:
  6.5 0.0 copy-start
  6.5 0.0 all-gather.4.cloned.1.call-start
  6.5 1.0 slice.16
  7.6 0.1 copy.22
  7.7 0.9 slice.15
  8.7 0.1 copy.21
  8.8 0.8 pad_maximum_fusion
  9.6 0.0 all-gather.4.cloned.1.call-update
  9.6 0.0 all-gather.6.cloned.1.call-start
  9.7 73.9 %all-gather.4.cloned.1.call-done = bf16[2,768,2048]{1,2,0:T(8,128)(2,1)} async-done(((bf16[2,768,128]{1,2,0:T(8,128)(2,1)}), bf16[2,768,2048]{1,2,0:T(8,128)(2,1)}) %all-gather.4.cloned.1.call-update) | async-done | bytes 6291472 | tf_op jit(solution)/shard_map/all_gather | solution.py:22
  83.6 0.0 copy-done
  83.6 9.7 convert_bitcast_fusion
  93.3 8.7 copy.16
  102.0 0.0 all-gather.6.cloned.1.call-update
  102.0 0.2 reduce-scatter.2.cloned.1.call-start
  102.2 0.7 constant_dynamic-slice_fusion
  103.0 0.1 slice.17
  103.1 0.5 broadcast_in_dim.2
  103.5 5.6 copy.25
  109.1 6.8 copy.18
  115.9 2020.0 %all-gather.6.cloned.1.call-done = bf16[32,768,2048]{2,1,0:T(8,128)(2,1)} async-done(((bf16[2,768,2048]{2,1,0:T(8,128)(2,1)}), bf16[32,768,2048]{2,1,0:T(8,128)(2,1)}) %all-gather.6.cloned.1.call-update) | async-done | bytes 100663312 | tf_op jit(solution)/shard_map/all_gather | solution.py:10
  2135.9 34.7 %reduce_sum.12 = bf16[2,768,2048]{2,1,0:T(8,128)(2,1)} reduce(bf16[16,2,768,2048]{3,2,1,0:T(8,128)(2,1)} %bitcast.4, bf16[]{:T(256)} %constant.5.clone.1), dimensions={0}, to_apply=%region_0.0 | reduce | flops 47185920 | bytes 106954752 | tf_op jit(solution)/shard_map/reduce_sum | solution.py:11
  2170.6 8.6 copy.20
  2179.3 0.0 copy-start.3
  2179.3 8.5 multiply_convert_fusion
  2187.8 0.0 copy-done.3
  2187.8 0.0 copy-start.2
  2187.8 0.0 copy-start.4
  2187.8 4.7 fusion
  2192.5 0.0 copy-done.2
  2192.5 0.0 copy-done.4
  2192.5 0.0 copy-start.1
  2192.5 4.1 fusion.1
  2196.6 0.0 reduce-scatter.2.cloned.1.call-update
  2196.6 82.9 %reduce-scatter.2.cloned.1.call-done = bf16[768,128]{0,1:T(8,128)(2,1)} async-done(((bf16[768,2048]{0,1:T(8,128)(2,1)}), bf16[768,128]{0,1:T(8,128)(2,1)}) %reduce-scatter.2.cloned.1.call-update) | async-done | bytes 196624 | tf_op jit(solution)/shard_map/reduce_scatter | solution.py:39
  2279.6 1.7 copy.19
  2281.3 0.0 copy-done.1
  (1 shorter events, 0.0 us)
Async XLA Ops:
  6.5 77.0 %copy-start = (bf16[768,768]{1,0:T(8,128)(2,1)S(1)}, bf16[768,768]{1,0:T(8,128)(2,1)}, u32[]{:S(2)}) copy-start(bf16[768,768]{1,0:T(8,128)(2,1)} %param.5) | copy-start | bytes 3538948
  6.5 77.0 %all-gather.4.cloned.1.call-start = ((), (), s32[]{:S(2)}) async-start(), calls=%async_computation.1 | async-start | bytes 6684672 | tf_op jit(solution)/shard_map/all_gather | solution.py:22
  9.6 2126.3 %all-gather.6.cloned.1.call-start = ((), (), s32[]{:S(2)}) async-start(), calls=%async_computation.3 | async-start | bytes 106954752 | tf_op jit(solution)/shard_map/all_gather | solution.py:10
  102.0 2177.6 %reduce-scatter.2.cloned.1.call-start = ((), (), s32[]{:S(2)}) async-start(), calls=%async_computation.2 | async-start | bytes 3342336 | tf_op jit(solution)/shard_map/reduce_scatter | solution.py:39
  2179.3 8.5 copy-start.3
  2187.8 4.8 copy-start.2
  2187.8 4.8 copy-start.4
  2192.5 88.8 %copy-start.1 = (bf16[768,768]{1,0:T(8,128)(2,1)S(1)}, bf16[768,768]{1,0:T(8,128)(2,1)}, u32[]{:S(2)}) copy-start(bf16[768,768]{1,0:T(8,128)(2,1)} %param.5) | copy-start | bytes 3538948
Sparse Core Ops, SparseCore 0:
  10.2 73.3 all-gather.3
  102.1 2033.7 all-gather.5
  2196.8 82.7 reduce-scatter.1
